TPU v7x, 512 devices: a whole 4x4x16 slice. The times are simulated.
512 devices in a mesh: space: 128 (over y, z, x_lo), dp: 4 (over x_hi, core).
Axes of the slice: x: 4 (x_hi: 2, x_lo: 2; x = x_hi * 2 + x_lo), y: 4, z: 16, core: 2. Of those that a mesh axis runs over, the one named last changes fastest.
Arguments:
- features: bfloat16 [4, 4096, 4, 128], P('dp', 'space'), may hold values from -6 to 6
- offsets: float32 [4, 4096, 3, 4], P('dp', 'space'), may hold values from 0 to 1
- counts: int32 [4, 4096], P('dp', 'space'), may hold values from 1 to 4
- in_weight: bfloat16 [128, 128], replicated, may hold values from -0.5 to 0.5
- mid_weight: bfloat16 [128, 128], replicated, may hold values from -0.5 to 0.5
- out_weight: bfloat16 [128, 128], replicated, may hold values from -0.5 to 0.5
- rbf_weight: bfloat16 [25, 128], replicated, may hold values from -4 to 4
- filter_weight: bfloat16 [128, 128], replicated, may hold values from -0.5 to 0.5
- readout: bfloat16 [128], replicated, may hold values from -6 to 6
- target: float32 [4], P('dp'), may hold values from -4 to 4
Outputs:
- updated: bfloat16 [4, 4096, 4, 128], P('dp', 'space')
- grad_in: float32 [128, 128], replicated
- grad_mid: float32 [128, 128], replicated
- grad_out: float32 [128, 128], replicated
- grad_rbf: float32 [25, 128], replicated
- grad_filter: float32 [128, 128], replicated
Inputs may be any that keep to these rules, and one draw needn't show every extreme that they name: The number of occupied slots of each cell, slots 0 to counts - 1 being occupied.
All inputs are finite; a program needn't handle non-finite values.
Results may differ from a plain program's by a relative error of at most 0.0069.
Values may be sent and summed in bfloat16 or wider, within the bound.
No kernel may reach another device: no remote copies, remote signals or barrier semaphores. Data moves between devices by JAX's collectives and lax.ppermute only.
A program may use at most 64 MiB of HBM per device.

v0:
```python
import math

import jax
import jax.numpy as jnp
from jax import lax
from jax.sharding import PartitionSpec as P

K = 25
BX = 2
BY = 4
BZ = 4
DEV_X = 1
DEV_Y = 2
DEV_Z = 4


cutoff = 1.0
block_cells = 8


def passed_along(value, axis, steps):
    count = lax.axis_size(axis)
    pairs = [(source, (source + steps) % count) for source in range(count)]
    return lax.ppermute(value, axis, pairs)


def shifted_ssp(values):
    return jax.nn.softplus(values) - math.log(2.0)


def pair_tile(window_geometry, rbf_weight, filter_weight):
    slot_count = window_geometry.shape[2]
    centre = jnp.arange(27)
    cell_shift = jnp.stack([centre // 9 - 1, centre // 3 % 3 - 1, centre % 3 - 1], axis=1).astype(
        jnp.float32
    )
    own_places = window_geometry[13, :3, :]
    neighbour_places = window_geometry[:, :3, :] + cell_shift[:, :, None]
    separation = neighbour_places[None, :, :, :] - jnp.transpose(own_places)[:, None, :, None]
    distance = jnp.sqrt(jnp.sum(separation * separation, axis=2))
    slots_here = jnp.arange(slot_count)
    itself = (centre[None, :, None] == 13) & (
        slots_here[None, None, :] == slots_here[:, None, None]
    )
    inside = (distance < cutoff) & jnp.logical_not(itself)
    smooth = 0.5 * (jnp.cos(math.pi * distance / cutoff) + 1.0)
    weight = jnp.where(inside, smooth, 0.0) * window_geometry[None, :, 3, :]
    distance = distance.reshape(-1)
    weight = weight.reshape(-1)
    centers = jnp.arange(K).astype(jnp.float32) * (cutoff / (K - 1))
    sharpness = (K - 1) * (K - 1) / 2.0
    gaussians = jnp.exp(-sharpness * (distance[None, :] - centers[:, None]) ** 2).astype(
        jnp.bfloat16
    )
    pre_filter = lax.dot_general(
        gaussians, rbf_weight, (((0,), (0,)), ((), ())), preferred_element_type=jnp.float32
    )
    squashed = shifted_ssp(pre_filter).astype(jnp.bfloat16)
    filter_base = jnp.dot(squashed, filter_weight, preferred_element_type=jnp.float32)
    filters = (filter_base * weight[:, None]).astype(jnp.bfloat16)
    return (gaussians, pre_filter, squashed, filters, weight)


def cell_window(extended, pos_x, pos_y, pos_z):
    corner = (pos_x, pos_y, pos_z) + (0,) * (extended.ndim - 3)
    shape_out = (3, 3, 3) + extended.shape[3:]
    return lax.dynamic_slice(extended, corner, shape_out).reshape((27,) + extended.shape[3:])


def extend_brick(brick, strides, sender):
    for axis_pos in range(3):
        extent = brick.shape[axis_pos]
        rims = []
        for direction in (1, -1):
            layer = extent - 1 if direction == 1 else 0
            rim_piece = lax.slice_in_dim(brick, layer, layer + 1, axis=axis_pos)
            rims.append(sender(rim_piece, direction * strides[axis_pos]))
        brick = jnp.concatenate([rims[0], brick, rims[1]], axis=axis_pos)
    return brick


def fold_back(accumulator, strides, sender):
    for axis_pos in (2, 1, 0):
        extent = accumulator.shape[axis_pos]
        inner_part = lax.slice_in_dim(accumulator, 1, extent - 1, axis=axis_pos)
        for direction in (1, -1):
            layer = extent - 1 if direction == 1 else 0
            target_layer = 0 if direction == 1 else extent - 3
            rim_piece = lax.slice_in_dim(accumulator, layer, layer + 1, axis=axis_pos)
            received = sender(rim_piece, direction * strides[axis_pos])
            current = lax.slice_in_dim(inner_part, target_layer, target_layer + 1, axis=axis_pos)
            inner_part = lax.dynamic_update_slice_in_dim(
                inner_part, current + received, target_layer, axis=axis_pos
            )
        accumulator = inner_part
    return accumulator


def shards(
    features,
    offsets,
    counts,
    in_weight,
    mid_weight,
    out_weight,
    rbf_weight,
    filter_weight,
    readout,
    target,
):
    strides = (DEV_X, DEV_Y, DEV_Z)
    cell_count = features.shape[1]
    slot_count = features.shape[2]
    feature_width = features.shape[3]
    occupied = (jnp.arange(slot_count)[None, :] < counts[0][:, None]).astype(jnp.float32)
    geometry = jnp.concatenate([offsets[0], occupied[:, None, :]], axis=1).reshape(
        BX, BY, BZ, 4, slot_count
    )

    def geometry_send(rim_piece, moved_by):
        return passed_along(rim_piece, "space", moved_by)

    def feature_send(rim_piece, moved_by):
        return passed_along(rim_piece, "space", moved_by)

    def sums_send(rim_piece, moved_by):
        return passed_along(rim_piece, "space", moved_by)

    geometry_ext = extend_brick(geometry, strides, geometry_send)
    flat_features = features[0].reshape(cell_count * slot_count, feature_width)
    hidden = jnp.dot(flat_features, in_weight, preferred_element_type=jnp.float32).astype(
        jnp.bfloat16
    )
    widened = extend_brick(
        hidden.reshape(BX, BY, BZ, slot_count, feature_width), strides, feature_send
    )
    step_total = cell_count // block_cells
    block_offsets = jnp.arange(block_cells)

    def locate(step_index):
        cell_ids = step_index * block_cells + block_offsets
        return (cell_ids // (BY * BZ), cell_ids // BZ % BY, cell_ids % BZ)

    def forward_cell(pos_x, pos_y, pos_z):
        window_geometry = cell_window(geometry_ext, pos_x, pos_y, pos_z)
        pieces = pair_tile(window_geometry, rbf_weight, filter_weight)
        filters = pieces[3].reshape(slot_count, 27 * slot_count, feature_width)
        sources = cell_window(widened, pos_x, pos_y, pos_z).reshape(27 * slot_count, feature_width)
        return jnp.einsum("jf,ijf->if", sources, filters, preferred_element_type=jnp.float32)

    def forward_step(step_index):
        pos_x, pos_y, pos_z = locate(step_index)
        return jax.vmap(forward_cell, in_axes=(0, 0, 0))(pos_x, pos_y, pos_z)

    message = lax.map(forward_step, jnp.arange(step_total)).reshape(
        cell_count * slot_count, feature_width
    )
    message_low = message.astype(jnp.bfloat16)
    inner = jnp.dot(message_low, mid_weight, preferred_element_type=jnp.float32)
    activation = shifted_ssp(inner).astype(jnp.bfloat16)
    updated = (
        flat_features.astype(jnp.float32)
        + jnp.dot(activation, out_weight, preferred_element_type=jnp.float32)
    ).astype(jnp.bfloat16)
    occupied_flat = occupied.reshape(-1)
    energy = jnp.dot(updated, readout, preferred_element_type=jnp.float32)
    energy_sum = jnp.sum(energy * occupied_flat)
    live_total = jnp.sum(occupied_flat)
    contract_rows = (((0,), (0,)), ((), ()))
    start_grad = (occupied_flat[:, None] * readout[None, :].astype(jnp.float32)).astype(
        jnp.bfloat16
    )
    grad_out = lax.dot_general(
        activation, start_grad, contract_rows, preferred_element_type=jnp.float32
    )
    back_act = lax.dot_general(
        start_grad, out_weight, (((1,), (1,)), ((), ())), preferred_element_type=jnp.float32
    )
    back_inner = (back_act * jax.nn.sigmoid(inner)).astype(jnp.bfloat16)
    grad_mid = lax.dot_general(
        message_low, back_inner, contract_rows, preferred_element_type=jnp.float32
    )
    cotangent = lax.dot_general(
        back_inner, mid_weight, (((1,), (1,)), ((), ())), preferred_element_type=jnp.float32
    ).astype(jnp.bfloat16)
    cotangent_brick = cotangent.reshape(BX, BY, BZ, slot_count, feature_width)

    def pair_backward(pos_x, pos_y, pos_z):
        window_geometry = cell_window(geometry_ext, pos_x, pos_y, pos_z)
        gaussians, pre_filter, squashed, filters, weight = pair_tile(
            window_geometry, rbf_weight, filter_weight
        )
        sources = cell_window(widened, pos_x, pos_y, pos_z).reshape(27 * slot_count, feature_width)
        own_cotangent = lax.dynamic_slice(
            cotangent_brick, (pos_x, pos_y, pos_z, 0, 0), (1, 1, 1, slot_count, feature_width)
        ).reshape(slot_count, feature_width)
        pair_grad = (
            (
                own_cotangent.astype(jnp.float32)[:, None, :]
                * sources.astype(jnp.float32)[None, :, :]
                * weight.reshape(slot_count, 27 * slot_count)[:, :, None]
            )
            .astype(jnp.bfloat16)
            .reshape(-1, feature_width)
        )
        filter_part = lax.dot_general(
            squashed, pair_grad, contract_rows, preferred_element_type=jnp.float32
        )
        back_squash = lax.dot_general(
            pair_grad, filter_weight, (((1,), (1,)), ((), ())), preferred_element_type=jnp.float32
        )
        back_pre = (back_squash * jax.nn.sigmoid(pre_filter)).astype(jnp.bfloat16)
        rbf_part = jnp.dot(gaussians, back_pre, preferred_element_type=jnp.float32)
        return (
            rbf_part,
            filter_part,
            filters.reshape(slot_count, 27 * slot_count, feature_width),
            own_cotangent,
            window_geometry[13, 3, :],
        )

    batched = jax.vmap(pair_backward, in_axes=(0, 0, 0))
    grad_start = (
        jnp.zeros((K, feature_width), jnp.float32),
        jnp.zeros((feature_width, feature_width), jnp.float32),
    )
    accumulator = jnp.zeros((BX + 2, BY + 2, BZ + 2, slot_count, feature_width), jnp.float32)

    def send_step(running, step_index):
        grad_rbf_now, grad_filter_now, gathered_sums = running
        pos_x, pos_y, pos_z = locate(step_index)
        rbf_part, filter_part, filters, own_cotangent, own_live = batched(pos_x, pos_y, pos_z)
        spread = jnp.einsum(
            "cif,cijf->cjf", own_cotangent, filters, preferred_element_type=jnp.float32
        )
        for member in range(block_cells):
            corner = (pos_x[member], pos_y[member], pos_z[member], 0, 0)
            current = lax.dynamic_slice(gathered_sums, corner, (3, 3, 3, slot_count, feature_width))
            gathered_sums = lax.dynamic_update_slice(
                gathered_sums,
                current + spread[member].reshape(3, 3, 3, slot_count, feature_width),
                corner,
            )
        return (
            (
                grad_rbf_now + jnp.sum(rbf_part, axis=0),
                grad_filter_now + jnp.sum(filter_part, axis=0),
                gathered_sums,
            ),
            None,
        )

    (grad_rbf, grad_filter, accumulator), unused = lax.scan(
        send_step, (grad_start[0], grad_start[1], accumulator), jnp.arange(step_total)
    )
    back_hidden = fold_back(accumulator, strides, sums_send)
    back_low = back_hidden.reshape(cell_count * slot_count, feature_width).astype(jnp.bfloat16)
    grad_in = lax.dot_general(
        flat_features, back_low, contract_rows, preferred_element_type=jnp.float32
    )
    statistics = lax.psum((energy_sum, live_total), "space")
    snapshot_scale = 2.0 * (statistics[0] / statistics[1] - target[0]) / statistics[1]
    totals = lax.psum(
        (
            snapshot_scale * grad_in,
            snapshot_scale * grad_mid,
            snapshot_scale * grad_out,
            snapshot_scale * grad_rbf,
            snapshot_scale * grad_filter,
        ),
        ("space", "dp"),
    )
    return (
        updated.reshape(1, cell_count, slot_count, feature_width),
        totals[0],
        totals[1],
        totals[2],
        totals[3],
        totals[4],
    )


def solution(mesh):
    placed = (
        P("dp", "space", None, None),
        P("dp", "space", None, None),
        P("dp", "space"),
        P(),
        P(),
        P(),
        P(),
        P(),
        P(),
        P("dp"),
    )
    return jax.shard_map(
        shards,
        mesh=mesh,
        in_specs=placed,
        out_specs=(P("dp", "space", None, None), P(), P(), P(), P(), P()),
        check_vma=False,
    )
```

profile of v0, /device:TPU:1, one launch (start us, length us, event | category | flops | bytes accessed | tf_op | source)
XLA Modules:
  0.0 1197.8 jit_solution(12709744172630294330)
XLA Ops:
  8.2 15.3 %collective-permute-start.7 = (bf16[1,4,4,4,128]{4,3,2,1,0:T(4,128)(2,1)S(1)}, bf16[1,4,4,4,128]{4,3,2,1,0:T(4,128)(2,1)S(1)}, u32[]{:S(2)}, u32[]{:S(2)}) collective-permute-start(bf16[1,4,4,4,128]{4,3,2,1,0:T(4,128)(2,1)S(1)} %bitcast.341), channel_id=1, source_target_pairs={{0,508},{4,0},{8,4},{12,8},{16,12},{20,16},{24,20},{28,24},{32,28}... | collective-permute-start | bytes 49160 | tf_op jit(solution)/shard_map/ppermute | solution.py:24
  27.0 7.6 collective-permute-start.1
  45.5 6.7 collective-permute-start.3
  54.2 6.7 collective-permute-start.9
  62.9 7.6 collective-permute-start.5
  72.5 7.6 collective-permute-start.11
  81.2 36.1 %while.32 = (s32[]{:T(128)}, bf16[4,8,4,128]{3,2,1,0:T(4,128)(2,1)S(1)}, s32[4]{0:T(128)S(1)}, f32[4,6,6,4,4]{4,3,2,1,0:T(4,128)S(1)}, bf16[25,128]{1,0:T(8,128)...) while((s32[]{:T(128)}, ...), condition=%wide.region_2.3_spmd.clone, body=%wide.region_0.2_spmd.clone.sunk | while | flops 145108016 | bytes 9560283 | solution.py:155
  87.4 2.4 multiply_convert_fusion.8
  96.4 2.4 multiply_convert_fusion.8
  105.4 2.4 multiply_convert_fusion.8
  114.5 2.4 multiply_convert_fusion.8
  119.3 256.6 %while.33 = (s32[]{:T(128)}, f32[25,128]{1,0:T(8,128)}, f32[128,128]{1,0:T(8,128)}, f32[4,6,6,4,128]{4,3,2,1,0:T(4,128)S(1)}, s32[4]{0:T(128)}, /*index=5*/f32[4...) while((s32[]{:T(128)}, f32[25,128]{1,0:T(8,128)}, ...), condition=%wide.region_9.10_spmd.clone, body=%wide.region_7.9_spmd.clone.sunk | while | flops 402532608 | bytes 24708872 | solution.py:253
  178.0 2.0 fusion.160
  241.5 2.9 fusion.160
  305.8 2.9 fusion.160
  370.1 2.9 fusion.160
  375.9 2.1 collective-permute-start.12
  380.2 250.3 %all-reduce.1 = (f32[]{:T(128)}, f32[]{:T(128)}) all-reduce(f32[]{:T(128)} %fusion.84, f32[]{:T(128)} %convert_reduce_fusion), channel_id=1, replica_groups=mesh['space'=128,'dp'=4] {'space'}, use_global_device_ids=true, to_apply=%region_4.5 | all-reduce | flops 2 | bytes 16 | tf_op jit(solution)/shard_map/psum | solution.py:261
  636.0 2.4 collective-permute-done.13
  642.0 6.7 collective-permute-start.15
  649.7 2.5 collective-permute-start.16
  652.9 7.0 collective-permute-start.17
  661.8 164.4 %psum.54 = f32[25,128]{1,0:T(8,128)} all-reduce(f32[25,128]{1,0:T(8,128)S(1)} %broadcast_multiply_fusion.2), channel_id=1, replica_groups=mesh['space'=128,'dp'=4] {'space','dp'}, use_global_device_ids=true, to_apply=%region_13.14 | all-reduce | flops 3200 | bytes 25600 | tf_op jit(solution)/shard_map/psum | solution.py:263
  826.2 358.7 %all-reduce.4.cloned.1.call-done = (f32[128,128]{0,1:T(8,128)}, f32[128,128]{1,0:T(8,128)}, f32[128,128]{1,0:T(8,128)}, f32[128,128]{1,0:T(8,128)}) async-done(((f32[128,128]{0,1:T(8,128)}, f32[128,128]{1,0:T(8,128)}, f32[128,128]{1,0:T(8,128)}, f32[128,128]{1,0:T(8,128)}), (f32[128,128]{0,1:T(8,128)}, f32[128,128]{1,0:T(8,128)}, f32[128,128]{1,0:T(8,128)}, ...) | async-done | bytes 262160 | tf_op jit(solution)/shard_map/psum | solution.py:263
  (584 shorter events, 127.1 us)
Async XLA Ops:
  7.2 110.3 %copy-start = (bf16[128,128]{1,0:T(8,128)(2,1)S(1)}, bf16[128,128]{1,0:T(8,128)(2,1)}, u32[]{:S(2)}) copy-start(bf16[128,128]{1,0:T(8,128)(2,1)} %param.19) | copy-start | bytes 98308
  7.2 1177.7 %all-reduce.4.cloned.1.call-start = ((), (), s32[]{:S(2)}) async-start(), calls=%async_computation | async-start | bytes 524288 | tf_op jit(solution)/shard_map/psum | solution.py:263
  8.2 44.1 %collective-permute-start.7 = (bf16[1,4,4,4,128]{4,3,2,1,0:T(4,128)(2,1)S(1)}, bf16[1,4,4,4,128]{4,3,2,1,0:T(4,128)(2,1)S(1)}, u32[]{:S(2)}, u32[]{:S(2)}) collective-permute-start(bf16[1,4,4,4,128]{4,3,2,1,0:T(4,128)(2,1)S(1)} %bitcast.341), channel_id=1, source_target_pairs={{0,508},{4,0},{8,4},{12,8},{16,12},{20,16},{24,20},{28,24},{32,28}... | collective-permute-start | bytes 49160 | tf_op jit(solution)/shard_map/ppermute | solution.py:24
  23.5 28.8 %collective-permute-start.6 = (bf16[1,4,4,4,128]{4,3,2,1,0:T(4,128)(2,1)S(1)}, bf16[1,4,4,4,128]{4,3,2,1,0:T(4,128)(2,1)S(1)}, u32[]{:S(2)}, u32[]{:S(2)}) collective-permute-start(bf16[1,4,4,4,128]{4,3,2,1,0:T(4,128)(2,1)S(1)} %bitcast.340), channel_id=1, source_target_pairs={{0,4},{4,8},{8,12},{12,16},{16,20},{20,24},{24,28},{28,32},{32,36}... | collective-permute-start | bytes 49160 | tf_op jit(solution)/shard_map/ppermute | solution.py:24
  27.0 15.3 %collective-permute-start.1 = (f32[1,4,4,4,4]{4,3,2,1,0:T(4,128)S(1)}, f32[1,4,4,4,4]{4,3,2,1,0:T(4,128)S(1)}, u32[]{:S(2)}, u32[]{:S(2)}) collective-permute-start(f32[1,4,4,4,4]{4,3,2,1,0:T(4,128)S(1)} %bitcast.337), channel_id=1, source_target_pairs={{0,508},{4,0},{8,4},{12,8},{16,12},{20,16},{24,20},{28,24},{32,28}... | collective-permute-start | bytes 3080 | tf_op jit(solution)/shard_map/ppermute | solution.py:24
  34.7 8.9 collective-permute-start
  42.2 76.1 %copy-start.17 = (f32[128]{0:T(128)}, f32[128]{0:T(128)S(1)}, u32[]{:S(2)}) copy-start(f32[128]{0:T(128)S(1)} %convert_element_type.202) | copy-start | bytes 1540
  43.6 17.3 %collective-permute-start.2 = (f32[4,1,4,4,4]{4,3,2,1,0:T(4,128)S(1)}, f32[4,1,4,4,4]{4,3,2,1,0:T(4,128)S(1)}, u32[]{:S(2)}, u32[]{:S(2)}) collective-permute-start(f32[4,1,4,4,4]{4,3,2,1,0:T(4,128)S(1)} %get-tuple-element.539), channel_id=1, source_target_pairs={{0,8},{4,12},{8,16},{12,20},{16,24},{20,28},{24,32},{28,36},{32,40... | collective-permute-start | bytes 3080 | tf_op jit(solution)/shard_map/ppermute | solution.py:24
  45.5 15.4 %collective-permute-start.3 = (f32[4,1,4,4,4]{4,3,2,1,0:T(4,128)S(1)}, f32[4,1,4,4,4]{4,3,2,1,0:T(4,128)S(1)}, u32[]{:S(2)}, u32[]{:S(2)}) collective-permute-start(f32[4,1,4,4,4]{4,3,2,1,0:T(4,128)S(1)} %get-tuple-element.540), channel_id=1, source_target_pairs={{0,504},{4,508},{8,0},{12,4},{16,8},{20,12},{24,16},{28,20},{32,24... | collective-permute-start | bytes 3080 | tf_op jit(solution)/shard_map/ppermute | solution.py:24
  52.3 18.2 %collective-permute-start.8 = (bf16[4,1,4,4,128]{4,3,2,1,0:T(4,128)(2,1)S(1)}, bf16[4,1,4,4,128]{4,3,2,1,0:T(4,128)(2,1)S(1)}, u32[]{:S(2)}, u32[]{:S(2)}) collective-permute-start(bf16[4,1,4,4,128]{4,3,2,1,0:T(4,128)(2,1)S(1)} %get-tuple-element.545), channel_id=1, source_target_pairs={{0,8},{4,12},{8,16},{12,20},{16,24},{20,28},{24,32},{28,36},{32,40... | collective-permute-start | bytes 49160 | tf_op jit(solution)/shard_map/ppermute | solution.py:24
  54.2 16.3 %collective-permute-start.9 = (bf16[4,1,4,4,128]{4,3,2,1,0:T(4,128)(2,1)S(1)}, bf16[4,1,4,4,128]{4,3,2,1,0:T(4,128)(2,1)S(1)}, u32[]{:S(2)}, u32[]{:S(2)}) collective-permute-start(bf16[4,1,4,4,128]{4,3,2,1,0:T(4,128)(2,1)S(1)} %get-tuple-element.546), channel_id=1, source_target_pairs={{0,504},{4,508},{8,0},{12,4},{16,8},{20,12},{24,16},{28,20},{32,24... | collective-permute-start | bytes 49160 | tf_op jit(solution)/shard_map/ppermute | solution.py:24
  61.0 19.1 %collective-permute-start.4 = (f32[4,6,1,4,4]{4,3,2,1,0:T(4,128)S(1)}, f32[4,6,1,4,4]{4,3,2,1,0:T(4,128)S(1)}, u32[]{:S(2)}, u32[]{:S(2)}) collective-permute-start(f32[4,6,1,4,4]{4,3,2,1,0:T(4,128)S(1)} %get-tuple-element.535), channel_id=1, source_target_pairs={{0,16},{4,20},{8,24},{12,28},{16,32},{20,36},{24,40},{28,44},{32,4... | collective-permute-start | bytes 4616 | tf_op jit(solution)/shard_map/ppermute | solution.py:24
  62.9 17.2 %collective-permute-start.5 = (f32[4,6,1,4,4]{4,3,2,1,0:T(4,128)S(1)}, f32[4,6,1,4,4]{4,3,2,1,0:T(4,128)S(1)}, u32[]{:S(2)}, u32[]{:S(2)}) collective-permute-start(f32[4,6,1,4,4]{4,3,2,1,0:T(4,128)S(1)} %get-tuple-element.536), channel_id=1, source_target_pairs={{0,496},{4,500},{8,504},{12,508},{16,0},{20,4},{24,8},{28,12},{32,... | collective-permute-start | bytes 4616 | tf_op jit(solution)/shard_map/ppermute | solution.py:24
  70.6 9.6 collective-permute-start.10
  72.5 8.5 collective-permute-start.11
  375.9 276.3 %copy-start.10 = (f32[128,128]{1,0:T(8,128)S(1)}, f32[128,128]{1,0:T(8,128)}, u32[]{:S(2)}) copy-start(f32[128,128]{1,0:T(8,128)} %get-tuple-element.355) | copy-start | bytes 196612
  375.9 285.0 %copy-start.6 = (bf16[1,32,4,128]{3,2,1,0:T(4,128)(2,1)S(1)}, bf16[1,32,4,128]{3,2,1,0:T(4,128)(2,1)}, u32[]{:S(2)}) copy-start(bf16[1,32,4,128]{3,2,1,0:T(4,128)(2,1)} %param.14) | copy-start | bytes 98308
  375.9 285.9 %copy-start.13 = (f32[25,128]{1,0:T(8,128)S(1)}, f32[25,128]{1,0:T(8,128)}, u32[]{:S(2)}) copy-start(f32[25,128]{1,0:T(8,128)} %get-tuple-element.354) | copy-start | bytes 38404
  375.9 256.4 %collective-permute-start.12 = (f32[4,6,1,4,128]{4,3,2,1,0:T(4,128)S(1)}, f32[4,6,1,4,128]{4,3,2,1,0:T(4,128)S(1)}, u32[]{:S(2)}, u32[]{:S(2)}) collective-permute-start(f32[4,6,1,4,128]{4,3,2,1,0:T(4,128)S(1)} %slice.380), channel_id=1, source_target_pairs={{0,16},{4,20},{8,24},{12,28},{16,32},{20,36},{24,40},{28,44},{32,4... | collective-permute-start | bytes 147464 | tf_op jit(solution)/shard_map/ppermute | solution.py:24
  632.4 6.0 collective-permute-start.13
  638.5 10.2 collective-permute-start.14
  642.0 7.7 collective-permute-start.15
  649.7 10.2 collective-permute-start.16
  652.9 8.0 collective-permute-start.17
  (32 other events, 472.4 us)
Sparse Core Ops, SparseCore 0:
  661.9 522.9 all-reduce.3
where the time goes:
time: 1200 us
  blocking collectives  415 us (35%)
  waiting for transfers between devices  365 us (30%)
  loops' own time  188 us (16%)
  starting transfers between devices  85 us (7%)
  local copies, waits for them, and re-layouts  58.8 us (5%)
  matrix products  45.5 us (4%)
  other arithmetic  23.7 us (2%)
  between operations  17.1 us (1%)
    psum x1, waiting for transfers between devices, shards(): lax.psum((snapshot_scale * grad_in, snapshot_scale * grad_mid, snapshot_s...  359 us
    psum x1, blocking collectives, shards(): statistics = lax.psum((energy_sum, live_total), 'space')  250 us
    another operation x1, loops' own time, shards(): lax.scan(send_step, (grad_start[0], grad_start[1], accumulator), jnp.aran...  184 us
    psum x1, blocking collectives, shards(): lax.psum((snapshot_scale * grad_in, snapshot_scale * grad_mid, snapshot_s...  164 us
    ppermute x18, starting transfers between devices, passed_along(): return lax.ppermute(value, axis, pairs)  85 us
  transfers between devices with their start and end apart: 19, of which 6 were waited for; matrix products, arithmetic and copies ran while one was open for 1% of the time, Pallas kernels for 0%

commit v1 on v0

--- a/solution.py
+++ b/solution.py
@@ -94,6 +94,39 @@
             )
         accumulator = inner_part
     return accumulator
+
+
+def split_parts(value):
+    high = lax.reduce_precision(value, 8, 7)
+    middle = lax.reduce_precision(value - high, 8, 7)
+    low = lax.reduce_precision(value - high - middle, 8, 7)
+    return [high, middle, low]
+
+
+def reduced_gradients(rows, grad_rbf, energy_sum, live_total, target):
+    both = ("space", "dp")
+    space_count = lax.axis_size("space")
+    snaps = lax.axis_size("dp")
+    devices = space_count * snaps
+    width = rows.shape[1]
+    extra = jnp.pad(grad_rbf.reshape(-1, 8), ((0, devices - K * width // 8), (0, 0)))
+    facts = jnp.stack(split_parts(energy_sum) + split_parts(target) + [live_total])
+    facts = jnp.broadcast_to(jnp.pad(facts, (0, width - 15))[None, :], (devices, width - 8))
+    second = jnp.concatenate([extra, facts], axis=1)
+    sent = jnp.stack([rows, second], axis=1).astype(jnp.bfloat16)
+    got = lax.all_to_all(sent, both, 0, 0, tiled=True).astype(jnp.float32)
+    per_snapshot = jnp.sum(got.reshape(space_count, snaps, 2, width), axis=0)
+    energy = jnp.sum(per_snapshot[:, 1, 8:11], axis=1)
+    live = per_snapshot[:, 1, 14]
+    targets = jnp.sum(got.reshape(space_count, snaps, 2, width)[0, :, 1, 11:14], axis=1)
+    factor = 2.0 * (energy / live - targets) / live
+    finished = jnp.sum(per_snapshot * factor[:, None, None], axis=0).astype(jnp.bfloat16)
+    back = lax.all_to_all(
+        jnp.broadcast_to(finished[None], (devices, 2, width)), both, 0, 0, tiled=True
+    ).astype(jnp.float32)
+    full = back[:, 0, :].reshape(4, width, width)
+    rbf = back[: K * width // 8, 1, :8].reshape(K, width)
+    return full[0], full[1], full[2], rbf, full[3]
 
 
 def shards(
@@ -258,18 +291,8 @@
     grad_in = lax.dot_general(
         flat_features, back_low, contract_rows, preferred_element_type=jnp.float32
     )
-    statistics = lax.psum((energy_sum, live_total), "space")
-    snapshot_scale = 2.0 * (statistics[0] / statistics[1] - target[0]) / statistics[1]
-    totals = lax.psum(
-        (
-            snapshot_scale * grad_in,
-            snapshot_scale * grad_mid,
-            snapshot_scale * grad_out,
-            snapshot_scale * grad_rbf,
-            snapshot_scale * grad_filter,
-        ),
-        ("space", "dp"),
-    )
+    rows = jnp.concatenate([grad_in, grad_mid, grad_out, grad_filter], axis=0)
+    totals = reduced_gradients(rows, grad_rbf, energy_sum, live_total, target[0])
     return (
         updated.reshape(1, cell_count, slot_count, feature_width),
         totals[0],

time: 1200 us -> 511 us (0.43)
  waiting for transfers between devices: 365 us -> 9.63 us
  blocking collectives: 415 us -> 78.9 us
    psum x2 -> x0, blocking collectives: 415 us -> none  [the longest x1 250 us: shards(): statistics = lax.psum((energy_sum, live_total), 'space')]
    psum x1 -> x0, waiting for transfers between devices: 359 us -> none  [shards(): lax.psum((snapshot_scale * grad_in, snapshot_scale * grad_mid, snapshot_s...]
    all_to_all x0 -> x2, blocking collectives: none -> 78.9 us  [the longest x1 45 us: reduced_gradients(): got = lax.all_to_all(sent, both, 0, 0, tiled=True).astype(jnp.float32)]
  transfers between devices with their start and end apart: 19 -> 18, of which waited for: 6 -> 5; matrix products, arithmetic and copies ran while one was open for 1% -> 3% of each run, Pallas kernels for 0% -> 0%
where the time goes in v1:
time: 511 us; the launch traced here: 506 us
  loops' own time  192 us (38%)
  starting transfers between devices  87.6 us (17%)
  blocking collectives  78.9 us (15%)
  local copies, waits for them, and re-layouts  60.9 us (12%)
  matrix products  43.6 us (9%)
  other arithmetic  24.7 us (5%)
  waiting for transfers between devices  9.63 us (2%)
  between operations  9.13 us (2%)
    another operation x1, loops' own time, shards(): lax.scan(send_step, (grad_start[0], grad_start[1], accumulator), jnp.aran...  188 us
    ppermute x18, starting transfers between devices, passed_along(): return lax.ppermute(value, axis, pairs)  87.6 us
    all_to_all x1, blocking collectives, reduced_gradients(): got = lax.all_to_all(sent, both, 0, 0, tiled=True).astype(jnp.float32)  45 us
    all_to_all x1, blocking collectives, reduced_gradients(): lax.all_to_all(jnp.broadcast_to(finished[None], (devices, 2, width)), bot...  33.9 us
    dot_general x8, matrix products, pair_tile(): jnp.dot(squashed, filter_weight, preferred_element_type=jnp.float32)  16 us
    gather x20, local copies, waits for them, and re-layouts, cell_window(): lax.dynamic_slice(extended, corner, shape_out)  13.1 us
    dot_general x4, matrix products, pair_backward(): lax.dot_general(squashed, pair_grad, contract_rows, preferred_element_typ...  10.7 us
  transfers between devices with their start and end apart: 18, of which 5 were waited for; matrix products, arithmetic and copies ran while one was open for 3% of the time, Pallas kernels for 0%

profile of v1, /device:TPU:1, one launch (start us, length us, event | category | flops | bytes accessed | tf_op | source)
XLA Modules:
  0.0 506.1 jit_solution(16758130253385089641)
XLA Ops:
  1.6 15.3 %collective-permute-start.7 = (bf16[1,4,4,4,128]{4,3,2,1,0:T(4,128)(2,1)S(1)}, bf16[1,4,4,4,128]{4,3,2,1,0:T(4,128)(2,1)S(1)}, u32[]{:S(2)}, u32[]{:S(2)}) collective-permute-start(bf16[1,4,4,4,128]{4,3,2,1,0:T(4,128)(2,1)S(1)} %bitcast.366), channel_id=1, source_target_pairs={{0,508},{4,0},{8,4},{12,8},{16,12},{20,16},{24,20},{28,24},{32,28}... | collective-permute-start | bytes 49160 | tf_op jit(solution)/shard_map/ppermute | solution.py:24
  20.5 7.6 %collective-permute-start.1 = (f32[1,4,4,4,4]{4,3,2,1,0:T(4,128)S(1)}, f32[1,4,4,4,4]{4,3,2,1,0:T(4,128)S(1)}, u32[]{:S(2)}, u32[]{:S(2)}) collective-permute-start(f32[1,4,4,4,4]{4,3,2,1,0:T(4,128)S(1)} %bitcast.362), channel_id=1, source_target_pairs={{0,508},{4,0},{8,4},{12,8},{16,12},{20,16},{24,20},{28,24},{32,28}... | collective-permute-start | bytes 3080 | tf_op jit(solution)/shard_map/ppermute | solution.py:24
  41.4 6.7 %collective-permute-start.3 = (f32[4,1,4,4,4]{4,3,2,1,0:T(4,128)S(1)}, f32[4,1,4,4,4]{4,3,2,1,0:T(4,128)S(1)}, u32[]{:S(2)}, u32[]{:S(2)}) collective-permute-start(f32[4,1,4,4,4]{4,3,2,1,0:T(4,128)S(1)} %get-tuple-element.502), channel_id=1, source_target_pairs={{0,504},{4,508},{8,0},{12,4},{16,8},{20,12},{24,16},{28,20},{32,24... | collective-permute-start | bytes 3080 | tf_op jit(solution)/shard_map/ppermute | solution.py:24
  50.1 6.7 %collective-permute-start.9 = (bf16[4,1,4,4,128]{4,3,2,1,0:T(4,128)(2,1)S(1)}, bf16[4,1,4,4,128]{4,3,2,1,0:T(4,128)(2,1)S(1)}, u32[]{:S(2)}, u32[]{:S(2)}) collective-permute-start(bf16[4,1,4,4,128]{4,3,2,1,0:T(4,128)(2,1)S(1)} %get-tuple-element.508), channel_id=1, source_target_pairs={{0,504},{4,508},{8,0},{12,4},{16,8},{20,12},{24,16},{28,20},{32,24... | collective-permute-start | bytes 49160 | tf_op jit(solution)/shard_map/ppermute | solution.py:24
  58.8 7.6 %collective-permute-start.5 = (f32[4,6,1,4,4]{4,3,2,1,0:T(4,128)S(1)}, f32[4,6,1,4,4]{4,3,2,1,0:T(4,128)S(1)}, u32[]{:S(2)}, u32[]{:S(2)}) collective-permute-start(f32[4,6,1,4,4]{4,3,2,1,0:T(4,128)S(1)} %get-tuple-element.498), channel_id=1, source_target_pairs={{0,496},{4,500},{8,504},{12,508},{16,0},{20,4},{24,8},{28,12},{32,... | collective-permute-start | bytes 4616 | tf_op jit(solution)/shard_map/ppermute | solution.py:24
  68.4 7.6 %collective-permute-start.11 = (bf16[4,6,1,4,128]{4,3,2,1,0:T(4,128)(2,1)S(1)}, bf16[4,6,1,4,128]{4,3,2,1,0:T(4,128)(2,1)S(1)}, u32[]{:S(2)}, u32[]{:S(2)}) collective-permute-start(bf16[4,6,1,4,128]{4,3,2,1,0:T(4,128)(2,1)S(1)} %get-tuple-element.506), channel_id=1, source_target_pairs={{0,496},{4,500},{8,504},{12,508},{16,0},{20,4},{24,8},{28,12},{32,... | collective-permute-start | bytes 73736 | tf_op jit(solution)/shard_map/ppermute | solution.py:24
  77.1 36.1 %while.32 = (s32[]{:T(128)}, bf16[4,8,4,128]{3,2,1,0:T(4,128)(2,1)S(1)}, s32[4]{0:T(128)S(1)}, f32[4,6,6,4,4]{4,3,2,1,0:T(4,128)S(1)}, bf16[25,128]{1,0:T(8,128)...) while((s32[]{:T(128)}, ...), condition=%wide.region_2.3_spmd.clone, body=%wide.region_0.2_spmd.clone.sunk | while | flops 145108016 | bytes 9560283 | solution.py:188
  83.3 2.4 multiply_convert_fusion.8
  92.3 2.4 multiply_convert_fusion.8
  101.3 2.4 multiply_convert_fusion.8
  110.4 2.4 multiply_convert_fusion.8
  115.2 261.3 %while.33 = (s32[]{:T(128)}, f32[25,128]{1,0:T(8,128)}, f32[128,128]{1,0:T(8,128)}, f32[4,6,6,4,128]{4,3,2,1,0:T(4,128)S(1)}, s32[4]{0:T(128)}, /*index=5*/f32[4...) while((s32[]{:T(128)}, f32[25,128]{1,0:T(8,128)}, ...), condition=%wide.region_5.6_spmd.clone, body=%wide.region_3.5_spmd.clone.sunk | while | flops 402532608 | bytes 24708872 | solution.py:286
  239.7 2.9 fusion.165
  305.2 2.9 fusion.165
  370.7 2.9 fusion.165
  376.4 2.1 collective-permute-start.12
  379.6 6.4 %collective-permute-done.12 = f32[4,6,1,4,128]{4,3,2,1,0:T(4,128)S(1)} collective-permute-done((f32[4,6,1,4,128]{4,3,2,1,0:T(4,128)S(1)}, f32[4,6,1,4,128]{4,3,2,1,0:T(4,128)S(1)}, u32[]{:S(2)}, u32[]{:S(2)}) %collective-permute-start.12) | collective-permute-done | bytes 49184 | tf_op jit(solution)/shard_map/ppermute | solution.py:24
  386.0 4.2 collective-permute-start.13
  399.3 4.5 stack.56
  403.9 6.7 %collective-permute-start.15 = (f32[4,1,4,4,128]{4,3,2,1,0:T(4,128)S(1)}, f32[4,1,4,4,128]{4,3,2,1,0:T(4,128)S(1)}, u32[]{:S(2)}, u32[]{:S(2)}) collective-permute-start(f32[4,1,4,4,128]{4,3,2,1,0:T(4,128)S(1)} %get-tuple-element.499), channel_id=1, source_target_pairs={{0,504},{4,508},{8,0},{12,4},{16,8},{20,12},{24,16},{28,20},{32,24... | collective-permute-start | bytes 98312 | tf_op jit(solution)/shard_map/ppermute | solution.py:24
  411.6 3.1 collective-permute-start.16
  415.0 6.7 %collective-permute-start.17 = (f32[1,4,4,4,128]{4,3,2,1,0:T(4,128)S(1)}, f32[1,4,4,4,128]{4,3,2,1,0:T(4,128)S(1)}, u32[]{:S(2)}, u32[]{:S(2)}) collective-permute-start(f32[1,4,4,4,128]{4,3,2,1,0:T(4,128)S(1)} %get-tuple-element.503), channel_id=1, source_target_pairs={{0,508},{4,0},{8,4},{12,8},{16,12},{20,16},{24,20},{28,24},{32,28}... | collective-permute-start | bytes 98312 | tf_op jit(solution)/shard_map/ppermute | solution.py:24
  423.3 45.0 %all_to_all.10 = bf16[512,2,128]{2,1,0:T(2,128)(2,1)S(1)} all-to-all(bf16[512,2,128]{2,1,0:T(2,128)(2,1)S(1)} %copy.198), channel_id=1, replica_groups=mesh['space'=128,'dp'=4] {'space','dp'}, dimensions={0} | all-to-all | bytes 524288 | tf_op jit(solution)/shard_map/all_to_all | solution.py:117
  469.8 33.9 %all_to_all.11 = bf16[512,2,128]{2,1,0:T(2,128)(2,1)S(1)} all-to-all(bf16[512,2,128]{2,1,0:T(2,128)(2,1)S(1)} %broadcast_in_dim.43), channel_id=1, replica_groups=mesh['space'=128,'dp'=4] {'space','dp'}, dimensions={0} | all-to-all | bytes 524288 | tf_op jit(solution)/shard_map/all_to_all | solution.py:124
  (598 shorter events, 123.2 us)
Async XLA Ops:
  0.6 112.8 %copy-start = (bf16[128,128]{1,0:T(8,128)(2,1)S(1)}, bf16[128,128]{1,0:T(8,128)(2,1)}, u32[]{:S(2)}) copy-start(bf16[128,128]{1,0:T(8,128)(2,1)} %param.19) | copy-start | bytes 98308
  0.6 76.4 %copy-start.1 = (bf16[25,128]{1,0:T(8,128)(2,1)S(1)}, bf16[25,128]{1,0:T(8,128)(2,1)}, u32[]{:S(2)}) copy-start(bf16[25,128]{1,0:T(8,128)(2,1)} %param.20) | copy-start | bytes 19204
  1.6 46.5 %collective-permute-start.7 = (bf16[1,4,4,4,128]{4,3,2,1,0:T(4,128)(2,1)S(1)}, bf16[1,4,4,4,128]{4,3,2,1,0:T(4,128)(2,1)S(1)}, u32[]{:S(2)}, u32[]{:S(2)}) collective-permute-start(bf16[1,4,4,4,128]{4,3,2,1,0:T(4,128)(2,1)S(1)} %bitcast.366), channel_id=1, source_target_pairs={{0,508},{4,0},{8,4},{12,8},{16,12},{20,16},{24,20},{28,24},{32,28}... | collective-permute-start | bytes 49160 | tf_op jit(solution)/shard_map/ppermute | solution.py:24
  16.9 31.2 %collective-permute-start.6 = (bf16[1,4,4,4,128]{4,3,2,1,0:T(4,128)(2,1)S(1)}, bf16[1,4,4,4,128]{4,3,2,1,0:T(4,128)(2,1)S(1)}, u32[]{:S(2)}, u32[]{:S(2)}) collective-permute-start(bf16[1,4,4,4,128]{4,3,2,1,0:T(4,128)(2,1)S(1)} %bitcast.365), channel_id=1, source_target_pairs={{0,4},{4,8},{8,12},{12,16},{16,20},{20,24},{24,28},{28,32},{32,36}... | collective-permute-start | bytes 49160 | tf_op jit(solution)/shard_map/ppermute | solution.py:24
  20.5 19.0 %collective-permute-start.1 = (f32[1,4,4,4,4]{4,3,2,1,0:T(4,128)S(1)}, f32[1,4,4,4,4]{4,3,2,1,0:T(4,128)S(1)}, u32[]{:S(2)}, u32[]{:S(2)}) collective-permute-start(f32[1,4,4,4,4]{4,3,2,1,0:T(4,128)S(1)} %bitcast.362), channel_id=1, source_target_pairs={{0,508},{4,0},{8,4},{12,8},{16,12},{20,16},{24,20},{28,24},{32,28}... | collective-permute-start | bytes 3080 | tf_op jit(solution)/shard_map/ppermute | solution.py:24
  28.1 11.3 %collective-permute-start = (f32[1,4,4,4,4]{4,3,2,1,0:T(4,128)S(1)}, f32[1,4,4,4,4]{4,3,2,1,0:T(4,128)S(1)}, u32[]{:S(2)}, u32[]{:S(2)}) collective-permute-start(f32[1,4,4,4,4]{4,3,2,1,0:T(4,128)S(1)} %bitcast.363), channel_id=1, source_target_pairs={{0,4},{4,8},{8,12},{12,16},{16,20},{20,24},{24,28},{28,32},{32,36}... | collective-permute-start | bytes 3080 | tf_op jit(solution)/shard_map/ppermute | solution.py:24
  39.3 74.9 %copy-start.17 = (f32[128]{0:T(128)}, f32[128]{0:T(128)S(1)}, u32[]{:S(2)}) copy-start(f32[128]{0:T(128)S(1)} %convert_element_type.217) | copy-start | bytes 1540
  39.4 74.8 %copy-start.18 = (f32[128]{0:T(128)}, f32[128]{0:T(128)S(1)}, u32[]{:S(2)}) copy-start(f32[128]{0:T(128)S(1)} %convert_element_type.216) | copy-start | bytes 1540
  39.5 17.3 %collective-permute-start.2 = (f32[4,1,4,4,4]{4,3,2,1,0:T(4,128)S(1)}, f32[4,1,4,4,4]{4,3,2,1,0:T(4,128)S(1)}, u32[]{:S(2)}, u32[]{:S(2)}) collective-permute-start(f32[4,1,4,4,4]{4,3,2,1,0:T(4,128)S(1)} %get-tuple-element.501), channel_id=1, source_target_pairs={{0,8},{4,12},{8,16},{12,20},{16,24},{20,28},{24,32},{28,36},{32,40... | collective-permute-start | bytes 3080 | tf_op jit(solution)/shard_map/ppermute | solution.py:24
  41.4 15.4 %collective-permute-start.3 = (f32[4,1,4,4,4]{4,3,2,1,0:T(4,128)S(1)}, f32[4,1,4,4,4]{4,3,2,1,0:T(4,128)S(1)}, u32[]{:S(2)}, u32[]{:S(2)}) collective-permute-start(f32[4,1,4,4,4]{4,3,2,1,0:T(4,128)S(1)} %get-tuple-element.502), channel_id=1, source_target_pairs={{0,504},{4,508},{8,0},{12,4},{16,8},{20,12},{24,16},{28,20},{32,24... | collective-permute-start | bytes 3080 | tf_op jit(solution)/shard_map/ppermute | solution.py:24
  48.2 18.2 %collective-permute-start.8 = (bf16[4,1,4,4,128]{4,3,2,1,0:T(4,128)(2,1)S(1)}, bf16[4,1,4,4,128]{4,3,2,1,0:T(4,128)(2,1)S(1)}, u32[]{:S(2)}, u32[]{:S(2)}) collective-permute-start(bf16[4,1,4,4,128]{4,3,2,1,0:T(4,128)(2,1)S(1)} %get-tuple-element.507), channel_id=1, source_target_pairs={{0,8},{4,12},{8,16},{12,20},{16,24},{20,28},{24,32},{28,36},{32,40... | collective-permute-start | bytes 49160 | tf_op jit(solution)/shard_map/ppermute | solution.py:24
  50.1 16.3 %collective-permute-start.9 = (bf16[4,1,4,4,128]{4,3,2,1,0:T(4,128)(2,1)S(1)}, bf16[4,1,4,4,128]{4,3,2,1,0:T(4,128)(2,1)S(1)}, u32[]{:S(2)}, u32[]{:S(2)}) collective-permute-start(bf16[4,1,4,4,128]{4,3,2,1,0:T(4,128)(2,1)S(1)} %get-tuple-element.508), channel_id=1, source_target_pairs={{0,504},{4,508},{8,0},{12,4},{16,8},{20,12},{24,16},{28,20},{32,24... | collective-permute-start | bytes 49160 | tf_op jit(solution)/shard_map/ppermute | solution.py:24
  56.9 19.1 %collective-permute-start.4 = (f32[4,6,1,4,4]{4,3,2,1,0:T(4,128)S(1)}, f32[4,6,1,4,4]{4,3,2,1,0:T(4,128)S(1)}, u32[]{:S(2)}, u32[]{:S(2)}) collective-permute-start(f32[4,6,1,4,4]{4,3,2,1,0:T(4,128)S(1)} %get-tuple-element.497), channel_id=1, source_target_pairs={{0,16},{4,20},{8,24},{12,28},{16,32},{20,36},{24,40},{28,44},{32,4... | collective-permute-start | bytes 4616 | tf_op jit(solution)/shard_map/ppermute | solution.py:24
  58.8 17.2 %collective-permute-start.5 = (f32[4,6,1,4,4]{4,3,2,1,0:T(4,128)S(1)}, f32[4,6,1,4,4]{4,3,2,1,0:T(4,128)S(1)}, u32[]{:S(2)}, u32[]{:S(2)}) collective-permute-start(f32[4,6,1,4,4]{4,3,2,1,0:T(4,128)S(1)} %get-tuple-element.498), channel_id=1, source_target_pairs={{0,496},{4,500},{8,504},{12,508},{16,0},{20,4},{24,8},{28,12},{32,... | collective-permute-start | bytes 4616 | tf_op jit(solution)/shard_map/ppermute | solution.py:24
  66.5 9.6 %collective-permute-start.10 = (bf16[4,6,1,4,128]{4,3,2,1,0:T(4,128)(2,1)S(1)}, bf16[4,6,1,4,128]{4,3,2,1,0:T(4,128)(2,1)S(1)}, u32[]{:S(2)}, u32[]{:S(2)}) collective-permute-start(bf16[4,6,1,4,128]{4,3,2,1,0:T(4,128)(2,1)S(1)} %get-tuple-element.505), channel_id=1, source_target_pairs={{0,16},{4,20},{8,24},{12,28},{16,32},{20,36},{24,40},{28,44},{32,4... | collective-permute-start | bytes 73736 | tf_op jit(solution)/shard_map/ppermute | solution.py:24
  68.4 8.5 %collective-permute-start.11 = (bf16[4,6,1,4,128]{4,3,2,1,0:T(4,128)(2,1)S(1)}, bf16[4,6,1,4,128]{4,3,2,1,0:T(4,128)(2,1)S(1)}, u32[]{:S(2)}, u32[]{:S(2)}) collective-permute-start(bf16[4,6,1,4,128]{4,3,2,1,0:T(4,128)(2,1)S(1)} %get-tuple-element.506), channel_id=1, source_target_pairs={{0,496},{4,500},{8,504},{12,508},{16,0},{20,4},{24,8},{28,12},{32,... | collective-permute-start | bytes 73736 | tf_op jit(solution)/shard_map/ppermute | solution.py:24
  115.4 51.6 %copy-start.2 = (bf16[2,4,4,4,128]{4,3,2,1,0:T(4,128)(2,1)}, bf16[2,4,4,4,128]{4,3,2,1,0:T(4,128)(2,1)S(1)}, u32[]{:S(2)}) copy-start(bf16[2,4,4,4,128]{4,3,2,1,0:T(4,128)(2,1)S(1)} %get-tuple-element.782) | copy-start | bytes 98308 | tf_op jit(solution)/shard_map/while
  311.0 51.6 %copy-start.2 = (bf16[2,4,4,4,128]{4,3,2,1,0:T(4,128)(2,1)}, bf16[2,4,4,4,128]{4,3,2,1,0:T(4,128)(2,1)S(1)}, u32[]{:S(2)}) copy-start(bf16[2,4,4,4,128]{4,3,2,1,0:T(4,128)(2,1)S(1)} %get-tuple-element.782) | copy-start | bytes 98308 | tf_op jit(solution)/shard_map/while
  376.4 9.5 %collective-permute-start.12 = (f32[4,6,1,4,128]{4,3,2,1,0:T(4,128)S(1)}, f32[4,6,1,4,128]{4,3,2,1,0:T(4,128)S(1)}, u32[]{:S(2)}, u32[]{:S(2)}) collective-permute-start(f32[4,6,1,4,128]{4,3,2,1,0:T(4,128)S(1)} %slice.413), channel_id=1, source_target_pairs={{0,16},{4,20},{8,24},{12,28},{16,32},{20,36},{24,40},{28,44},{32,4... | collective-permute-start | bytes 147464 | tf_op jit(solution)/shard_map/ppermute | solution.py:24
  386.0 5.7 %collective-permute-start.13 = (f32[4,6,1,4,128]{4,3,2,1,0:T(4,128)S(1)}, f32[4,6,1,4,128]{4,3,2,1,0:T(4,128)S(1)}, u32[]{:S(2)}, u32[]{:S(2)}) collective-permute-start(f32[4,6,1,4,128]{4,3,2,1,0:T(4,128)S(1)} %get-tuple-element.491), channel_id=1, source_target_pairs={{0,496},{4,500},{8,504},{12,508},{16,0},{20,4},{24,8},{28,12},{32,... | collective-permute-start | bytes 147464 | tf_op jit(solution)/shard_map/ppermute | solution.py:24
  391.8 18.8 %collective-permute-start.14 = (f32[4,1,4,4,128]{4,3,2,1,0:T(4,128)S(1)}, f32[4,1,4,4,128]{4,3,2,1,0:T(4,128)S(1)}, u32[]{:S(2)}, u32[]{:S(2)}) collective-permute-start(f32[4,1,4,4,128]{4,3,2,1,0:T(4,128)S(1)} %get-tuple-element.500), channel_id=1, source_target_pairs={{0,8},{4,12},{8,16},{12,20},{16,24},{20,28},{24,32},{28,36},{32,40... | collective-permute-start | bytes 98312 | tf_op jit(solution)/shard_map/ppermute | solution.py:24
  403.9 7.7 %collective-permute-start.15 = (f32[4,1,4,4,128]{4,3,2,1,0:T(4,128)S(1)}, f32[4,1,4,4,128]{4,3,2,1,0:T(4,128)S(1)}, u32[]{:S(2)}, u32[]{:S(2)}) collective-permute-start(f32[4,1,4,4,128]{4,3,2,1,0:T(4,128)S(1)} %get-tuple-element.499), channel_id=1, source_target_pairs={{0,504},{4,508},{8,0},{12,4},{16,8},{20,12},{24,16},{28,20},{32,24... | collective-permute-start | bytes 98312 | tf_op jit(solution)/shard_map/ppermute | solution.py:24
  411.6 10.1 %collective-permute-start.16 = (f32[1,4,4,4,128]{4,3,2,1,0:T(4,128)S(1)}, f32[1,4,4,4,128]{4,3,2,1,0:T(4,128)S(1)}, u32[]{:S(2)}, u32[]{:S(2)}) collective-permute-start(f32[1,4,4,4,128]{4,3,2,1,0:T(4,128)S(1)} %get-tuple-element.504), channel_id=1, source_target_pairs={{0,4},{4,8},{8,12},{12,16},{16,20},{20,24},{24,28},{28,32},{32,36}... | collective-permute-start | bytes 98312 | tf_op jit(solution)/shard_map/ppermute | solution.py:24
  415.0 7.7 %collective-permute-start.17 = (f32[1,4,4,4,128]{4,3,2,1,0:T(4,128)S(1)}, f32[1,4,4,4,128]{4,3,2,1,0:T(4,128)S(1)}, u32[]{:S(2)}, u32[]{:S(2)}) collective-permute-start(f32[1,4,4,4,128]{4,3,2,1,0:T(4,128)S(1)} %get-tuple-element.503), channel_id=1, source_target_pairs={{0,508},{4,0},{8,4},{12,8},{16,12},{20,16},{24,20},{28,24},{32,28}... | collective-permute-start | bytes 98312 | tf_op jit(solution)/shard_map/ppermute | solution.py:24
  (31 other events, 345.8 us)

commit v2 on v1

v2 whole, which is shorter than its diff:
```python
import math

import jax
import jax.numpy as jnp
from jax import lax
from jax.experimental import pallas as pl
from jax.experimental.pallas import tpu as pltpu
from jax.sharding import PartitionSpec as P

K = 25
BX = 2
BY = 4
BZ = 4
DEV_X = 1
DEV_Y = 2
DEV_Z = 4


CELLS = 32
LANES = 128
PAIRS = 112
cutoff = 1.0


def passed_along(value, axis, steps):
    count = lax.axis_size(axis)
    pairs = [(source, (source + steps) % count) for source in range(count)]
    return lax.ppermute(value, axis, pairs)


def extend_brick(brick, strides, sender):
    for axis_pos in range(3):
        extent = brick.shape[axis_pos]
        rims = []
        for direction in (1, -1):
            layer = extent - 1 if direction == 1 else 0
            rim_piece = lax.slice_in_dim(brick, layer, layer + 1, axis=axis_pos)
            rims.append(sender(rim_piece, direction * strides[axis_pos]))
        brick = jnp.concatenate([rims[0], brick, rims[1]], axis=axis_pos)
    return brick


def column_of(values, mask):
    return jnp.sum(jnp.where(mask, values, 0.0), axis=1, keepdims=True)


def dot_rows(left, right):
    return lax.dot_general(
        left, right, (((0,), (0,)), ((), ())), preferred_element_type=jnp.float32
    )


def dot_last(left, right):
    return lax.dot_general(
        left, right, (((1,), (1,)), ((), ())), preferred_element_type=jnp.float32
    )


def softplus_half(values):
    return jnp.maximum(values, 0.0) + jnp.log(1.0 + jnp.exp(-jnp.abs(values))) - math.log(2.0)


def logistic(values):
    return 0.5 * jnp.tanh(0.5 * values) + 0.5


def brick_kernel(
    wide_ref,
    own_ref,
    geo_ref,
    in_ref,
    mid_ref,
    out_ref,
    rbf_ref,
    filter_ref,
    readout_ref,
    updated_ref,
    rows_ref,
    grad_rbf_ref,
    energy_ref,
    hidden_ext,
    feature_ext,
    hidden_win,
    feature_win,
    gathered,
    expanded,
    distance_ref,
    omega_ref,
    gauss_ref,
    squashed_ref,
    slope_ref,
    filters_ref,
    product_ref,
    message_ref,
    cotangent_ref,
    grad_ref,
    pre_ref,
    spread_ref,
):
    f32 = jnp.float32
    bf16 = jnp.bfloat16
    feature_ext[...] = wide_ref[...].astype(f32)
    hidden_ext[...] = (
        jnp.dot(wide_ref[...], in_ref[...], preferred_element_type=f32).astype(bf16).astype(f32)
    )
    pad = jnp.zeros((LANES - 108, LANES), f32)
    for cell in range(CELLS):
        pos_x, pos_y, pos_z = cell // 16, cell // 4 % 4, cell % 4
        for member in range(9):
            start = ((pos_x + member // 3) * 6 + pos_y + member % 3) * 24 + 4 * pos_z
            place = cell * LANES + 12 * member
            hidden_win[place : place + 12, :] = hidden_ext[start : start + 12, :]
            feature_win[place : place + 12, :] = feature_ext[start : start + 12, :]
        hidden_win[cell * LANES + 108 : (cell + 1) * LANES, :] = pad
        feature_win[cell * LANES + 108 : (cell + 1) * LANES, :] = pad

    total = jnp.zeros((32, 4 * LANES), f32)
    source = lax.broadcasted_iota(jnp.int32, (24, 4 * LANES), 0)
    column = lax.broadcasted_iota(jnp.int32, (24, 4 * LANES), 1)
    lane_of = column % LANES
    for member in range(9):
        pos_x, pos_y = member // 3, member % 3
        local = lane_of - 12 * member
        chosen = (local >= 0) & (local < 12) & (source == 4 * (column // LANES) + local)
        picked = jnp.concatenate(
            [
                geo_ref[pos_x * 24 + pos_y * 4 : pos_x * 24 + pos_y * 4 + 16, :],
                geo_ref[(pos_x + 1) * 24 + pos_y * 4 : (pos_x + 1) * 24 + pos_y * 4 + 16, :],
            ],
            axis=0,
        )
        total = total + jnp.dot(
            picked,
            jnp.where(chosen, 1.0, 0.0).astype(f32),
            preferred_element_type=f32,
            precision=lax.Precision.HIGHEST,
        )
    gathered[...] = total
    for cell in range(CELLS):
        for part in range(4):
            row = (cell // 4) * 4 + part
            here = cell % 4 * LANES
            expanded[part, 4 * cell : 4 * cell + 4, :] = jnp.broadcast_to(
                gathered[row : row + 1, here : here + LANES], (4, LANES)
            )
    lane = lax.broadcasted_iota(jnp.int32, (LANES, LANES), 1)
    slot = lax.broadcasted_iota(jnp.int32, (LANES, LANES), 0) % 4
    itself = lane == 52 + slot
    member = lane // 12
    shifts = (member // 3 - 1, member % 3 - 1, lane % 12 // 4 - 1)
    squares = jnp.zeros((LANES, LANES), f32)
    for part in range(3):
        places = expanded[part]
        own = column_of(places, itself)
        separation = places + shifts[part].astype(f32) - own
        squares = squares + separation * separation
    distance = jnp.sqrt(squares)
    occupied = expanded[3]
    live = column_of(occupied, itself)
    inside = (distance < cutoff) & jnp.logical_not(itself) & (lane < 108)
    smooth = 0.5 * (jnp.cos(math.pi * distance / cutoff) + 1.0)
    omega = jnp.where(inside, smooth, 0.0) * occupied
    distance_ref[...] = distance
    omega_ref[...] = omega

    order = lax.broadcasted_iota(jnp.int32, (32, LANES), 0)
    centers = order.astype(f32) * (cutoff / (K - 1))
    sharpness = (K - 1) * (K - 1) / 2.0
    empty = jnp.zeros((LANES - PAIRS, LANES), bf16)

    def forward(cell, carry):
        tiles = []
        for slot_id in range(4):
            at = pl.ds(4 * cell + slot_id, 1)
            away = distance_ref[at, :] - centers
            tile = jnp.exp(-sharpness * away * away)
            weight = omega_ref[at, :]
            high = weight.astype(bf16).astype(f32)
            middle = (weight - high).astype(bf16).astype(f32)
            low = weight - high - middle
            extra = jnp.where(order == K, high, jnp.where(order == K + 1, middle, low))
            tiles.append(
                jnp.where(order < K, tile, jnp.where(order < K + 3, extra, 0.0)).astype(bf16)
            )
        gauss = jnp.concatenate(tiles, axis=1)
        gauss_ref[cell] = gauss
        both = dot_rows(gauss, rbf_ref[...])
        base_row = pl.multiple_of(cell * LANES, LANES)
        hidden = hidden_win[pl.ds(base_row, PAIRS), :]
        for slot_id in range(4):
            first = slot_id * LANES
            pre = both[first : first + PAIRS, :LANES]
            squashed = jnp.log(1.0 + jnp.exp(pre)) - math.log(2.0)
            squashed_ref[cell, first : first + PAIRS, :] = squashed.astype(bf16)
            squashed_ref[cell, first + PAIRS : first + LANES, :] = empty
            slope_ref[cell, first : first + PAIRS, :] = logistic(pre)
        base = jnp.dot(squashed_ref[cell], filter_ref[...], preferred_element_type=f32)
        for slot_id in range(4):
            first = slot_id * LANES
            weight = both[first : first + PAIRS, LANES:]
            filters = (base[first : first + PAIRS, :] * weight).astype(bf16)
            filters_ref[cell, first : first + PAIRS, :] = filters
            product_ref[cell, first : first + PAIRS, :] = hidden * weight
            message_ref[pl.ds(4 * cell + slot_id, 1), :] = jnp.sum(
                hidden * filters.astype(f32), axis=0, keepdims=True
            )
        return carry

    lax.fori_loop(0, CELLS, forward, 0)

    message = message_ref[...].astype(bf16)
    inner = jnp.dot(message, mid_ref[...], preferred_element_type=f32)
    activation = softplus_half(inner).astype(bf16)
    updated = (
        own_ref[...].astype(f32) + jnp.dot(activation, out_ref[...], preferred_element_type=f32)
    ).astype(bf16)
    updated_ref[...] = updated
    readout = readout_ref[...].astype(f32)
    start_grad = (live * readout).astype(bf16)
    energy = jnp.sum(updated.astype(f32) * readout * live, axis=0, keepdims=True)
    energy_ref[...] = jnp.broadcast_to(energy, (8, LANES))
    rows_ref[2 * LANES : 3 * LANES, :] = dot_rows(activation, start_grad)
    back_inner = (dot_last(start_grad, out_ref[...]) * logistic(inner)).astype(bf16)
    rows_ref[LANES : 2 * LANES, :] = dot_rows(message, back_inner)
    cotangent_ref[...] = dot_last(back_inner, mid_ref[...]).astype(bf16).astype(f32)
    rows_ref[0:LANES, :] = jnp.zeros((LANES, LANES), f32)
    rows_ref[3 * LANES : 4 * LANES, :] = jnp.zeros((LANES, LANES), f32)
    grad_rbf_ref[...] = jnp.zeros((32, LANES), f32)
    spread_ref[...] = jnp.zeros((LANES, LANES), bf16)
    grad_ref[...] = jnp.zeros((4 * LANES, LANES), bf16)
    pre_ref[...] = jnp.zeros((4 * LANES, LANES), bf16)

    def backward(cell, carry):
        spread = jnp.zeros((PAIRS, LANES), f32)
        for slot_id in range(4):
            first = slot_id * LANES
            cotangent = cotangent_ref[pl.ds(4 * cell + slot_id, 1), :]
            grad_ref[first : first + PAIRS, :] = (
                cotangent * product_ref[cell, first : first + PAIRS, :]
            ).astype(bf16)
            spread = spread + cotangent * filters_ref[cell, first : first + PAIRS, :].astype(f32)
        spread_ref[0:PAIRS, :] = spread.astype(bf16)
        back = dot_last(grad_ref[...], filter_ref[...])
        for slot_id in range(4):
            first = slot_id * LANES
            pre_ref[first : first + PAIRS, :] = (
                back[first : first + PAIRS, :] * slope_ref[cell, first : first + PAIRS, :]
            ).astype(bf16)
        rows_ref[3 * LANES : 4 * LANES, :] += dot_rows(squashed_ref[cell], grad_ref[...])
        grad_rbf_ref[...] += jnp.dot(gauss_ref[cell], pre_ref[...], preferred_element_type=f32)
        base_row = pl.multiple_of(cell * LANES, LANES)
        rows_ref[0:LANES, :] += dot_rows(
            feature_win[pl.ds(base_row, LANES), :].astype(bf16), spread_ref[...]
        )
        return carry

    lax.fori_loop(0, CELLS, backward, 0)


def brick_pass(wide, own, geometry, in_weight, mid_weight, out_weight, rbf_weight, filter_weight, readout, interpret=False):
    f32 = jnp.float32
    bf16 = jnp.bfloat16
    left = jnp.pad(rbf_weight, ((0, 32 - K), (0, LANES)))
    ones = jnp.pad(jnp.ones((3, LANES), bf16), ((K, 32 - K - 3), (LANES, 0)))
    tall = CELLS * LANES
    return pl.pallas_call(
        brick_kernel,
        out_shape=(
            jax.ShapeDtypeStruct((LANES, LANES), bf16),
            jax.ShapeDtypeStruct((4 * LANES, LANES), f32),
            jax.ShapeDtypeStruct((32, LANES), f32),
            jax.ShapeDtypeStruct((8, LANES), f32),
        ),
        in_specs=[pl.BlockSpec(memory_space=pltpu.VMEM)] * 9,
        out_specs=[pl.BlockSpec(memory_space=pltpu.VMEM)] * 4,
        scratch_shapes=[
            pltpu.VMEM((576, LANES), f32),
            pltpu.VMEM((576, LANES), f32),
            pltpu.VMEM((tall, LANES), f32),
            pltpu.VMEM((tall, LANES), f32),
            pltpu.VMEM((32, 4 * LANES), f32),
            pltpu.VMEM((4, LANES, LANES), f32),
            pltpu.VMEM((LANES, LANES), f32),
            pltpu.VMEM((LANES, LANES), f32),
            pltpu.VMEM((CELLS, 32, 4 * LANES), bf16),
            pltpu.VMEM((CELLS, 4 * LANES, LANES), bf16),
            pltpu.VMEM((CELLS, 4 * LANES, LANES), f32),
            pltpu.VMEM((CELLS, 4 * LANES, LANES), bf16),
            pltpu.VMEM((CELLS, 4 * LANES, LANES), f32),
            pltpu.VMEM((LANES, LANES), f32),
            pltpu.VMEM((LANES, LANES), f32),
            pltpu.VMEM((4 * LANES, LANES), bf16),
            pltpu.VMEM((4 * LANES, LANES), bf16),
            pltpu.VMEM((LANES, LANES), bf16),
        ],
        compiler_params=pltpu.CompilerParams(vmem_limit_bytes=50 * 1024 * 1024),
        interpret=interpret,
    )(
        wide,
        own,
        geometry,
        in_weight,
        mid_weight,
        out_weight,
        left + ones,
        filter_weight,
        readout.reshape(1, LANES),
    )


def split_parts(value):
    high = lax.reduce_precision(value, 8, 7)
    middle = lax.reduce_precision(value - high, 8, 7)
    low = lax.reduce_precision(value - high - middle, 8, 7)
    return [high, middle, low]


def reduced_gradients(rows, grad_rbf, energy_sum, live_total, target):
    both = ("space", "dp")
    space_count = lax.axis_size("space")
    snaps = lax.axis_size("dp")
    devices = space_count * snaps
    width = rows.shape[1]
    extra = jnp.pad(grad_rbf.reshape(-1, 8), ((0, devices - K * width // 8), (0, 0)))
    facts = jnp.stack(split_parts(energy_sum) + split_parts(target) + [live_total])
    facts = jnp.broadcast_to(jnp.pad(facts, (0, width - 15))[None, :], (devices, width - 8))
    second = jnp.concatenate([extra, facts], axis=1)
    sent = jnp.stack([rows, second], axis=1).astype(jnp.bfloat16)
    got = lax.all_to_all(sent, both, 0, 0, tiled=True).astype(jnp.float32)
    per_snapshot = jnp.sum(got.reshape(space_count, snaps, 2, width), axis=0)
    energy = jnp.sum(per_snapshot[:, 1, 8:11], axis=1)
    live = per_snapshot[:, 1, 14]
    targets = jnp.sum(got.reshape(space_count, snaps, 2, width)[0, :, 1, 11:14], axis=1)
    factor = 2.0 * (energy / live - targets) / live
    finished = jnp.sum(per_snapshot * factor[:, None, None], axis=0).astype(jnp.bfloat16)
    back = lax.all_to_all(
        jnp.broadcast_to(finished[None], (devices, 2, width)), both, 0, 0, tiled=True
    ).astype(jnp.float32)
    full = back[:, 0, :].reshape(4, width, width)
    rbf = back[: K * width // 8, 1, :8].reshape(K, width)
    return full[0], full[1], full[2], rbf, full[3]


def shards(
    features,
    offsets,
    counts,
    in_weight,
    mid_weight,
    out_weight,
    rbf_weight,
    filter_weight,
    readout,
    target,
):
    strides = (DEV_X, DEV_Y, DEV_Z)
    cell_count = features.shape[1]
    slot_count = features.shape[2]
    feature_width = features.shape[3]
    occupied = (jnp.arange(slot_count)[None, :] < counts[0][:, None]).astype(jnp.float32)
    geometry = jnp.concatenate([offsets[0], occupied[:, None, :]], axis=1).reshape(
        BX, BY, BZ, 4, slot_count
    )

    def geometry_send(rim_piece, moved_by):
        return passed_along(rim_piece, "space", moved_by)

    def feature_send(rim_piece, moved_by):
        return passed_along(rim_piece, "space", moved_by)

    geometry_ext = extend_brick(geometry, strides, geometry_send)
    widened = extend_brick(
        features[0].reshape(BX, BY, BZ, slot_count, feature_width), strides, feature_send
    )
    live_total = jnp.sum(occupied)
    updated, rows, grad_rbf, energy = brick_pass(
        widened.reshape(-1, feature_width),
        features[0].reshape(cell_count * slot_count, feature_width),
        jnp.transpose(geometry_ext, (0, 1, 3, 2, 4)).reshape(96, 24),
        in_weight,
        mid_weight,
        out_weight,
        rbf_weight,
        filter_weight,
        readout,
    )
    energy_sum = jnp.sum(energy[0])
    grad_rbf = grad_rbf[:K]
    totals = reduced_gradients(rows, grad_rbf, energy_sum, live_total, target[0])
    return (
        updated.reshape(1, cell_count, slot_count, feature_width),
        totals[0],
        totals[1],
        totals[2],
        totals[3],
        totals[4],
    )


def solution(mesh):
    placed = (
        P("dp", "space", None, None),
        P("dp", "space", None, None),
        P("dp", "space"),
        P(),
        P(),
        P(),
        P(),
        P(),
        P(),
        P("dp"),
    )
    return jax.shard_map(
        shards,
        mesh=mesh,
        in_specs=placed,
        out_specs=(P("dp", "space", None, None), P(), P(), P(), P(), P()),
        check_vma=False,
    )
```

time: 511 us -> 193 us (0.38)
  loops' own time: 192 us -> 0 us
  local copies, waits for them, and re-layouts: 60.9 us -> 11 us
  matrix products: 43.6 us -> 0 us
  Pallas kernels: 0 us -> 29.4 us
  starting transfers between devices: 87.6 us -> 62.9 us
  other arithmetic: 24.7 us -> 4.65 us
  waiting for transfers between devices: 9.63 us -> 0.44 us
    another operation x2 -> x0, loops' own time: 192 us -> none  [the longest x1 188 us: shards(): lax.scan(send_step, (grad_start[0], grad_start[1], accumulator), jnp.aran...]
    dot_general x33 -> x0, matrix products: 43.6 us -> none  [the longest x8 16 us: pair_tile(): jnp.dot(squashed, filter_weight, preferred_element_type=jnp.float32)]
    pallas_call x0 -> x1, Pallas kernels: none -> 29.4 us  [brick_pass(): pl.pallas_call(brick_kernel, out_shape=(jax.ShapeDtypeStruct((LANES, LANE...]
    ppermute x18 -> x12, starting transfers between devices: 87.6 us -> 62.9 us  [passed_along(): return lax.ppermute(value, axis, pairs)]
    gather x24 -> x0, local copies, waits for them, and re-layouts: 15.6 us -> none  [the longest x20 13.1 us: cell_window(): lax.dynamic_slice(extended, corner, shape_out)]
    slice x30 -> x1, local copies, waits for them, and re-layouts: 10.5 us -> 0.01 us  [shards(): grad_rbf = grad_rbf[:K]]
    mul x20 -> x0, other arithmetic: 9.24 us -> none  [the longest x8 6.34 us: pair_tile(): weight = jnp.where(inside, smooth, 0.0) * window_geometry[None, :, 3, :]]
    ppermute x18 -> x12, waiting for transfers between devices: 9.63 us -> 0.44 us  [passed_along(): return lax.ppermute(value, axis, pairs)]
  transfers between devices with their start and end apart: 18 -> 12, of which waited for: 5 -> 1; matrix products, arithmetic and copies ran while one was open for 3% -> 2% of each run, Pallas kernels for 0% -> 0%
where the time goes in v2:
time: 193 us; the launch traced here: 192 us
  blocking collectives  75.3 us (39%)
  starting transfers between devices  62.9 us (33%)
  Pallas kernels  29.4 us (15%)
  local copies, waits for them, and re-layouts  11 us (6%)
  between operations  8.67 us (4%)
  other arithmetic  4.65 us (2%)
    ppermute x12, starting transfers between devices, passed_along(): return lax.ppermute(value, axis, pairs)  62.9 us
    all_to_all x1, blocking collectives, reduced_gradients(): got = lax.all_to_all(sent, both, 0, 0, tiled=True).astype(jnp.float32)  41.4 us
    all_to_all x1, blocking collectives, reduced_gradients(): lax.all_to_all(jnp.broadcast_to(finished[None], (devices, 2, width)), bot...  33.9 us
    pallas_call x1, Pallas kernels, brick_pass(): pl.pallas_call(brick_kernel, out_shape=(jax.ShapeDtypeStruct((LANES, LANE...  29.4 us
    another operation x1, local copies, waits for them, and re-layouts, reduced_gradients(): jnp.stack(split_parts(energy_sum) + split_parts(target) + [live_total])  4.57 us
  transfers between devices with their start and end apart: 12, of which 1 were waited for; matrix products, arithmetic and copies ran while one was open for 2% of the time, Pallas kernels for 0%

profile of v2, /device:TPU:1, one launch (start us, length us, event | category | flops | bytes accessed | tf_op | source)
XLA Modules:
  0.0 192.4 jit_solution(13901101173023589872)
XLA Ops:
  0.6 0.7 fusion.4
  1.7 3.9 %collective-permute-start.6 = (f32[1,4,4,4,4]{3,1,0,4,2:T(4,128)S(1)}, f32[1,4,4,4,4]{3,1,0,4,2:T(4,128)S(1)}, u32[]{:S(2)}, u32[]{:S(2)}) collective-permute-start(f32[1,4,4,4,4]{3,1,0,4,2:T(4,128)S(1)} %copy.42), channel_id=1, source_target_pairs={{0,4},{4,8},{8,12},{12,16},{16,20},{20,24},{24,28},{28,32},{32,36}... | collective-permute-start | bytes 3080 | tf_op jit(solution)/shard_map/ppermute | solution.py:28
  6.0 13.3 %collective-permute-start.7 = (f32[1,4,4,4,4]{3,1,0,4,2:T(4,128)S(1)}, f32[1,4,4,4,4]{3,1,0,4,2:T(4,128)S(1)}, u32[]{:S(2)}, u32[]{:S(2)}) collective-permute-start(f32[1,4,4,4,4]{3,1,0,4,2:T(4,128)S(1)} %copy.45), channel_id=1, source_target_pairs={{0,508},{4,0},{8,4},{12,8},{16,12},{20,16},{24,20},{28,24},{32,28}... | collective-permute-start | bytes 3080 | tf_op jit(solution)/shard_map/ppermute | solution.py:28
  19.3 1.9 collective-permute-start
  21.2 7.6 %collective-permute-start.1 = (bf16[1,4,4,4,128]{4,3,2,1,0:T(4,128)(2,1)S(1)}, bf16[1,4,4,4,128]{4,3,2,1,0:T(4,128)(2,1)S(1)}, u32[]{:S(2)}, u32[]{:S(2)}) collective-permute-start(bf16[1,4,4,4,128]{4,3,2,1,0:T(4,128)(2,1)S(1)} %bitcast.53), channel_id=1, source_target_pairs={{0,508},{4,0},{8,4},{12,8},{16,12},{20,16},{24,20},{28,24},{32,28}... | collective-permute-start | bytes 49160 | tf_op jit(solution)/shard_map/ppermute | solution.py:28
  29.3 0.7 reduce.12
  30.3 0.6 copy-done.7
  30.9 0.6 convert_reduce_fusion
  35.7 1.9 collective-permute-start.8
  37.6 6.7 %collective-permute-start.9 = (f32[4,1,4,4,4]{3,1,0,4,2:T(1,128)S(1)}, f32[4,1,4,4,4]{3,1,0,4,2:T(1,128)S(1)}, u32[]{:S(2)}, u32[]{:S(2)}) collective-permute-start(f32[4,1,4,4,4]{3,1,0,4,2:T(1,128)S(1)} %get-tuple-element.21), channel_id=1, source_target_pairs={{0,504},{4,508},{8,0},{12,4},{16,8},{20,12},{24,16},{28,20},{32,24... | collective-permute-start | bytes 3080 | tf_op jit(solution)/shard_map/ppermute | solution.py:28
  44.3 1.9 collective-permute-start.2
  46.3 6.7 %collective-permute-start.3 = (bf16[4,1,4,4,128]{4,3,2,1,0:T(4,128)(2,1)S(1)}, bf16[4,1,4,4,128]{4,3,2,1,0:T(4,128)(2,1)S(1)}, u32[]{:S(2)}, u32[]{:S(2)}) collective-permute-start(bf16[4,1,4,4,128]{4,3,2,1,0:T(4,128)(2,1)S(1)} %get-tuple-element.25), channel_id=1, source_target_pairs={{0,504},{4,508},{8,0},{12,4},{16,8},{20,12},{24,16},{28,20},{32,24... | collective-permute-start | bytes 49160 | tf_op jit(solution)/shard_map/ppermute | solution.py:28
  53.1 1.9 collective-permute-start.10
  55.0 7.6 %collective-permute-start.11 = (f32[4,6,1,4,4]{3,1,0,4,2:T(8,128)S(1)}, f32[4,6,1,4,4]{3,1,0,4,2:T(8,128)S(1)}, u32[]{:S(2)}, u32[]{:S(2)}) collective-permute-start(f32[4,6,1,4,4]{3,1,0,4,2:T(8,128)S(1)} %get-tuple-element.19), channel_id=1, source_target_pairs={{0,496},{4,500},{8,504},{12,508},{16,0},{20,4},{24,8},{28,12},{32,... | collective-permute-start | bytes 4616 | tf_op jit(solution)/shard_map/ppermute | solution.py:28
  62.7 1.9 collective-permute-start.4
  64.6 7.6 %collective-permute-start.5 = (bf16[4,6,1,4,128]{4,3,2,1,0:T(4,128)(2,1)S(1)}, bf16[4,6,1,4,128]{4,3,2,1,0:T(4,128)(2,1)S(1)}, u32[]{:S(2)}, u32[]{:S(2)}) collective-permute-start(bf16[4,6,1,4,128]{4,3,2,1,0:T(4,128)(2,1)S(1)} %get-tuple-element.23), channel_id=1, source_target_pairs={{0,496},{4,500},{8,504},{12,508},{16,0},{20,4},{24,8},{28,12},{32,... | collective-permute-start | bytes 73736 | tf_op jit(solution)/shard_map/ppermute | solution.py:28
  73.9 29.4 %shard_map.145 = (bf16[128,128]{1,0:T(8,128)(2,1)}, f32[512,128]{1,0:T(8,128)S(1)}, f32[32,128]{1,0:T(8,128)S(1)}, f32[8,128]{1,0:T(8,128)S(1)}) custom-call(bf16[576,128]{1,0:T(8,128)(2,1)S(1)} %bitcast.46, bf16[128,128]{1,0:T(8,128)(2,1)S(1)} %bitcast.45, f32[96,24]{1,0:T(8,128)S(1)} %copy.46.geo_ref, bf16[128,128]{1,0:T(8,128)(2,1)S(1)} %copy-done.1, ...), custom_call_target="tpu_custom_call" | custom-call | tf_op jit(solution)/shard_map/pallas_call | solution.py:266
  103.3 0.6 slice_reduce_fusion.3
  108.1 4.6 %stack.44 = bf16[7]{0:T(256)(128)(2,1)S(1)} concatenate(f32[1]{0:T(128)} %bitcast.11, f32[1]{0:T(128)} %bitcast.12, bf16[1]{0:T(256)(128)(2,1)} %bitcast.13, f32[1]{0:T(128)} %bitcast.15, f32[1]{0:T(128)} %bitcast.16, bf16[1]{0:T(256)(128)(2,1)} %bitcast.17, bf16[1]{0:T(256)(128)(2,1)} %bitcast.18), dimensions={0} | concatenate | bytes 36 | tf_op jit(solution)/shard_map/stack | solution.py:325
  113.3 41.4 %all_to_all.10 = bf16[512,2,128]{2,1,0:T(2,128)(2,1)S(1)} all-to-all(bf16[512,2,128]{2,1,0:T(2,128)(2,1)S(1)} %copy.47), channel_id=1, replica_groups=mesh['space'=128,'dp'=4] {'space','dp'}, dimensions={0} | all-to-all | bytes 524288 | tf_op jit(solution)/shard_map/all_to_all | solution.py:329
  156.0 33.9 %all_to_all.11 = bf16[512,2,128]{2,1,0:T(2,128)(2,1)S(1)} all-to-all(bf16[512,2,128]{2,1,0:T(2,128)(2,1)S(1)} %broadcast_in_dim.8), channel_id=1, replica_groups=mesh['space'=128,'dp'=4] {'space','dp'}, dimensions={0} | all-to-all | bytes 524288 | tf_op jit(solution)/shard_map/all_to_all | solution.py:336
  190.1 0.6 slice_reduce_fusion
  190.8 0.7 reshape_squeeze.12
  191.5 0.9 fusion.6
  (70 shorter events, 6.1 us)
Async XLA Ops:
  0.6 0.7 copy-start.6
  1.7 33.8 %collective-permute-start.6 = (f32[1,4,4,4,4]{3,1,0,4,2:T(4,128)S(1)}, f32[1,4,4,4,4]{3,1,0,4,2:T(4,128)S(1)}, u32[]{:S(2)}, u32[]{:S(2)}) collective-permute-start(f32[1,4,4,4,4]{3,1,0,4,2:T(4,128)S(1)} %copy.42), channel_id=1, source_target_pairs={{0,4},{4,8},{8,12},{12,16},{16,20},{20,24},{24,28},{28,32},{32,36}... | collective-permute-start | bytes 3080 | tf_op jit(solution)/shard_map/ppermute | solution.py:28
  5.7 13.5 %copy-start = (bf16[1,32,4,128]{3,2,1,0:T(4,128)(2,1)S(1)}, bf16[1,32,4,128]{3,2,1,0:T(4,128)(2,1)}, u32[]{:S(2)}) copy-start(bf16[1,32,4,128]{3,2,1,0:T(4,128)(2,1)} %param.10) | copy-start | bytes 98308
  6.0 29.6 %collective-permute-start.7 = (f32[1,4,4,4,4]{3,1,0,4,2:T(4,128)S(1)}, f32[1,4,4,4,4]{3,1,0,4,2:T(4,128)S(1)}, u32[]{:S(2)}, u32[]{:S(2)}) collective-permute-start(f32[1,4,4,4,4]{3,1,0,4,2:T(4,128)S(1)} %copy.45), channel_id=1, source_target_pairs={{0,508},{4,0},{8,4},{12,8},{16,12},{20,16},{24,20},{28,24},{32,28}... | collective-permute-start | bytes 3080 | tf_op jit(solution)/shard_map/ppermute | solution.py:28
  19.3 25.0 %collective-permute-start = (bf16[1,4,4,4,128]{4,3,2,1,0:T(4,128)(2,1)S(1)}, bf16[1,4,4,4,128]{4,3,2,1,0:T(4,128)(2,1)S(1)}, u32[]{:S(2)}, u32[]{:S(2)}) collective-permute-start(bf16[1,4,4,4,128]{4,3,2,1,0:T(4,128)(2,1)S(1)} %bitcast.54), channel_id=1, source_target_pairs={{0,4},{4,8},{8,12},{12,16},{16,20},{20,24},{24,28},{28,32},{32,36}... | collective-permute-start | bytes 49160 | tf_op jit(solution)/shard_map/ppermute | solution.py:28
  21.2 8.1 %copy-start.8 = (s32[1,32]{1,0:T(1,128)S(1)}, s32[1,32]{1,0:T(1,128)}, u32[]{:S(2)}) copy-start(s32[1,32]{1,0:T(1,128)} %param.12) | copy-start | bytes 388
  21.2 23.1 %collective-permute-start.1 = (bf16[1,4,4,4,128]{4,3,2,1,0:T(4,128)(2,1)S(1)}, bf16[1,4,4,4,128]{4,3,2,1,0:T(4,128)(2,1)S(1)}, u32[]{:S(2)}, u32[]{:S(2)}) collective-permute-start(bf16[1,4,4,4,128]{4,3,2,1,0:T(4,128)(2,1)S(1)} %bitcast.53), channel_id=1, source_target_pairs={{0,508},{4,0},{8,4},{12,8},{16,12},{20,16},{24,20},{28,24},{32,28}... | collective-permute-start | bytes 49160 | tf_op jit(solution)/shard_map/ppermute | solution.py:28
  30.2 0.7 copy-start.7
  35.7 17.3 %collective-permute-start.8 = (f32[4,1,4,4,4]{3,1,0,4,2:T(1,128)S(1)}, f32[4,1,4,4,4]{3,1,0,4,2:T(1,128)S(1)}, u32[]{:S(2)}, u32[]{:S(2)}) collective-permute-start(f32[4,1,4,4,4]{3,1,0,4,2:T(1,128)S(1)} %get-tuple-element.20), channel_id=1, source_target_pairs={{0,8},{4,12},{8,16},{12,20},{16,24},{20,28},{24,32},{28,36},{32,40... | collective-permute-start | bytes 3080 | tf_op jit(solution)/shard_map/ppermute | solution.py:28
  37.6 15.4 %collective-permute-start.9 = (f32[4,1,4,4,4]{3,1,0,4,2:T(1,128)S(1)}, f32[4,1,4,4,4]{3,1,0,4,2:T(1,128)S(1)}, u32[]{:S(2)}, u32[]{:S(2)}) collective-permute-start(f32[4,1,4,4,4]{3,1,0,4,2:T(1,128)S(1)} %get-tuple-element.21), channel_id=1, source_target_pairs={{0,504},{4,508},{8,0},{12,4},{16,8},{20,12},{24,16},{28,20},{32,24... | collective-permute-start | bytes 3080 | tf_op jit(solution)/shard_map/ppermute | solution.py:28
  44.3 18.3 %collective-permute-start.2 = (bf16[4,1,4,4,128]{4,3,2,1,0:T(4,128)(2,1)S(1)}, bf16[4,1,4,4,128]{4,3,2,1,0:T(4,128)(2,1)S(1)}, u32[]{:S(2)}, u32[]{:S(2)}) collective-permute-start(bf16[4,1,4,4,128]{4,3,2,1,0:T(4,128)(2,1)S(1)} %get-tuple-element.24), channel_id=1, source_target_pairs={{0,8},{4,12},{8,16},{12,20},{16,24},{20,28},{24,32},{28,36},{32,40... | collective-permute-start | bytes 49160 | tf_op jit(solution)/shard_map/ppermute | solution.py:28
  46.3 16.3 %collective-permute-start.3 = (bf16[4,1,4,4,128]{4,3,2,1,0:T(4,128)(2,1)S(1)}, bf16[4,1,4,4,128]{4,3,2,1,0:T(4,128)(2,1)S(1)}, u32[]{:S(2)}, u32[]{:S(2)}) collective-permute-start(bf16[4,1,4,4,128]{4,3,2,1,0:T(4,128)(2,1)S(1)} %get-tuple-element.25), channel_id=1, source_target_pairs={{0,504},{4,508},{8,0},{12,4},{16,8},{20,12},{24,16},{28,20},{32,24... | collective-permute-start | bytes 49160 | tf_op jit(solution)/shard_map/ppermute | solution.py:28
  53.1 19.1 %collective-permute-start.10 = (f32[4,6,1,4,4]{3,1,0,4,2:T(8,128)S(1)}, f32[4,6,1,4,4]{3,1,0,4,2:T(8,128)S(1)}, u32[]{:S(2)}, u32[]{:S(2)}) collective-permute-start(f32[4,6,1,4,4]{3,1,0,4,2:T(8,128)S(1)} %get-tuple-element.18), channel_id=1, source_target_pairs={{0,16},{4,20},{8,24},{12,28},{16,32},{20,36},{24,40},{28,44},{32,4... | collective-permute-start | bytes 4616 | tf_op jit(solution)/shard_map/ppermute | solution.py:28
  55.0 17.2 %collective-permute-start.11 = (f32[4,6,1,4,4]{3,1,0,4,2:T(8,128)S(1)}, f32[4,6,1,4,4]{3,1,0,4,2:T(8,128)S(1)}, u32[]{:S(2)}, u32[]{:S(2)}) collective-permute-start(f32[4,6,1,4,4]{3,1,0,4,2:T(8,128)S(1)} %get-tuple-element.19), channel_id=1, source_target_pairs={{0,496},{4,500},{8,504},{12,508},{16,0},{20,4},{24,8},{28,12},{32,... | collective-permute-start | bytes 4616 | tf_op jit(solution)/shard_map/ppermute | solution.py:28
  62.7 10.0 %collective-permute-start.4 = (bf16[4,6,1,4,128]{4,3,2,1,0:T(4,128)(2,1)S(1)}, bf16[4,6,1,4,128]{4,3,2,1,0:T(4,128)(2,1)S(1)}, u32[]{:S(2)}, u32[]{:S(2)}) collective-permute-start(bf16[4,6,1,4,128]{4,3,2,1,0:T(4,128)(2,1)S(1)} %get-tuple-element.22), channel_id=1, source_target_pairs={{0,16},{4,20},{8,24},{12,28},{16,32},{20,36},{24,40},{28,44},{32,4... | collective-permute-start | bytes 73736 | tf_op jit(solution)/shard_map/ppermute | solution.py:28
  64.6 8.5 %collective-permute-start.5 = (bf16[4,6,1,4,128]{4,3,2,1,0:T(4,128)(2,1)S(1)}, bf16[4,6,1,4,128]{4,3,2,1,0:T(4,128)(2,1)S(1)}, u32[]{:S(2)}, u32[]{:S(2)}) collective-permute-start(bf16[4,6,1,4,128]{4,3,2,1,0:T(4,128)(2,1)S(1)} %get-tuple-element.23), channel_id=1, source_target_pairs={{0,496},{4,500},{8,504},{12,508},{16,0},{20,4},{24,8},{28,12},{32,... | collective-permute-start | bytes 73736 | tf_op jit(solution)/shard_map/ppermute | solution.py:28
  72.7 0.8 copy-start.1
  72.7 0.8 copy-start.2
  72.7 0.8 copy-start.3
  72.7 0.8 copy-start.4
  73.3 0.7 copy-start.5
